TPU v7x, 32 devices: a whole 2x2x4 slice. The times are simulated.
32 devices in a mesh: group: 4 (over z), dom: 8 (over y, x, core).
Axes of the slice: x: 2, y: 2, z: 4, core: 2. Of those that a mesh axis runs over, the one named last changes fastest.
Arguments:
- hot_rows: bfloat16 [4096, 1024], P(('group', 'dom')), may hold values from -6 to 6
- cold_codes: bfloat16 [4096, 1024], P(('group', 'dom')), may hold values from -127 to 127
- scale_index: int32 [4096], P(('group', 'dom')), may hold values from 0 to 255
- scale_table: float32 [256], replicated, may hold values from 0.004 to 0.04
- stale_rows: bfloat16 [4096, 1024], P(('group', 'dom')), may hold values from -6 to 6
- tile_index: int32 [64, 3], P(('group', 'dom')), may hold values from 0 to 2
- tile_count: int32 [64], P(('group', 'dom')), may hold values from 1 to 3
- tile_values: bfloat16 [64, 3, 128, 128], P(('group', 'dom')), may hold values from -0.3125 to 0.3125
- weight: bfloat16 [1024, 1024], P('dom'), may hold values from -0.1875 to 0.1875
- out_grad: bfloat16 [8192, 1024], P(('group', 'dom')), may hold values from -6 to 6
- stale_grads: bfloat16 [4096, 1024], P(('group', 'dom')), may hold values from -6 to 6
- send_rows: int32 [256, 16], P(('group', 'dom')), may hold values from 0 to 255
Outputs:
- activations: bfloat16 [8192, 1024], P(('group', 'dom'))
- feature_grad: bfloat16 [8192, 1024], P(('group', 'dom'))
- weight_grad: float32 [1024, 1024], P('dom')
- next_rows: bfloat16 [4096, 1024], P(('group', 'dom'))
- next_grads: bfloat16 [4096, 1024], P(('group', 'dom'))
Inputs may be any that keep to these rules, and one draw needn't show every extreme that they name: `send_rows`: rows may repeat.
All inputs are finite; a program needn't handle non-finite values.
Results may differ from a plain program's by a relative error of at most 0.0061.
Values may be sent and summed in bfloat16 or wider, within the bound.
A program may use at most 64 MiB of HBM per device.

v0:
```python
import jax
import jax.numpy as jnp
from jax import lax
from jax.sharding import PartitionSpec as P


def dequantize(cold_codes, scale_index, scale_table):
    levels = jnp.arange(scale_table.shape[0], dtype=jnp.int32)
    lookup = jnp.sum(
        jnp.where(
            scale_index[:, None] == levels[None, :],
            scale_table[None, :],
            jnp.zeros_like(scale_table)[None, :],
        ),
        axis=1,
    )
    return (cold_codes.astype(jnp.float32) * lookup[:, None]).astype(jnp.bfloat16)


def silu_parts(preact):
    logistic = jax.nn.sigmoid(preact)
    return (preact * logistic, logistic * (1.0 + preact * (1.0 - logistic)))


def local(
    hot_rows,
    cold_codes,
    scale_index,
    scale_table,
    stale_rows,
    tile_index,
    tile_count,
    tile_values,
    weight,
    out_grad,
    stale_grads,
    send_rows,
):
    tile_slots = tile_values.shape[1]
    cluster_rows = tile_values.shape[2]
    local_rows = jnp.concatenate(
        [hot_rows, dequantize(cold_codes, scale_index, scale_table)], axis=0
    )
    row_count = local_rows.shape[0]
    sends = send_rows.reshape(-1)
    outgoing = jnp.take(local_rows, sends, axis=0)
    next_rows = lax.all_to_all(outgoing, "dom", split_axis=0, concat_axis=0, tiled=True)
    source = jnp.concatenate([local_rows, stale_rows], axis=0)
    src_count = source.shape[0] // cluster_rows
    live_mask = jnp.arange(tile_slots, dtype=jnp.int32)[None, :] < tile_count[:, None]
    masked = jnp.where(
        live_mask[:, :, None, None], tile_values, jnp.zeros_like(tile_values)
    ).astype(jnp.float32)
    selector = (
        tile_index[:, :, None] == jnp.arange(src_count, dtype=jnp.int32)[None, None, :]
    ).astype(jnp.float32)
    operator = jnp.einsum("ckj,ckab->cajb", selector, masked, precision=lax.Precision.HIGHEST)
    operator = operator.reshape(row_count, src_count * cluster_rows)
    hidden = jnp.dot(operator, source.astype(jnp.float32), precision=lax.Precision.HIGHEST)
    hidden = hidden.astype(jnp.bfloat16)
    preact = jnp.dot(
        hidden,
        lax.all_gather(weight, "dom", axis=0, tiled=True),
        preferred_element_type=jnp.float32,
    )
    activ, slope = silu_parts(preact)
    activations = activ.astype(jnp.bfloat16)
    pre_grad = (out_grad.astype(jnp.float32) * slope).astype(jnp.bfloat16)
    hid_grad = lax.dot_general(
        pre_grad,
        lax.all_gather(weight, "dom", axis=0, tiled=True),
        (((1,), (1,)), ((), ())),
        preferred_element_type=jnp.float32,
    )
    hid_grad = hid_grad.astype(jnp.bfloat16)
    partial_value = lax.dot_general(
        hidden, pre_grad, (((0,), (0,)), ((), ())), preferred_element_type=jnp.float32
    )
    block_sum = lax.psum_scatter(partial_value, "dom", scatter_dimension=0, tiled=True)
    weight_grad = lax.psum(block_sum, "group")
    src_grad = lax.dot_general(
        operator,
        hid_grad.astype(jnp.float32),
        (((0,), (0,)), ((), ())),
        precision=lax.Precision.HIGHEST,
    )
    bound_grad = src_grad[row_count:].astype(jnp.bfloat16)
    next_grads = lax.all_to_all(bound_grad, "dom", split_axis=0, concat_axis=0, tiled=True)
    placing = (jnp.arange(row_count, dtype=jnp.int32)[:, None] == sends[None, :]).astype(
        jnp.bfloat16
    )
    returned = jnp.dot(placing, stale_grads, preferred_element_type=jnp.float32)
    feature_grad = (src_grad[:row_count] + returned).astype(jnp.bfloat16)
    return (activations, feature_grad, weight_grad, next_rows, next_grads)


def solution(mesh):
    placed = (
        P(("group", "dom"), None),
        P(("group", "dom"), None),
        P(("group", "dom")),
        P(),
        P(("group", "dom"), None),
        P(("group", "dom"), None),
        P(("group", "dom")),
        P(("group", "dom"), None, None, None),
        P("dom", None),
        P(("group", "dom"), None),
        P(("group", "dom"), None),
        P(("group", "dom"), None),
    )
    return jax.shard_map(
        local,
        mesh=mesh,
        in_specs=placed,
        out_specs=(
            P(("group", "dom"), None),
            P(("group", "dom"), None),
            P("dom", None),
            P(("group", "dom"), None),
            P(("group", "dom"), None),
        ),
        check_vma=False,
    )
```

profile of v0, /device:TPU:0, one launch (start us, length us, event | category | flops | bytes accessed | tf_op | source)
XLA Modules:
  0.0 148.6 jit_solution(3321438472732656839)
XLA Ops:
  7.2 0.0 copy-start
  7.2 0.0 all-gather.2.cloned.1.call-start
  7.2 0.7 all-gather.2.cloned.1.call-update
  7.9 0.0 reduce-scatter.2.cloned.1.call-start
  8.0 0.9 select_reduce_fusion
  8.8 0.7 iota_compare_fusion.4
  9.6 1.0 broadcast_select_fusion.1
  10.6 1.1 multiply_convert_fusion.2
  11.6 1.0 fusion.11
  12.6 2.0 %convolution_convert_fusion = bf16[256,1024]{1,0:T(8,128)(2,1)S(1)} fusion(bf16[128,1024]{1,0:T(8,128)(2,1)} %param.16, bf16[128,1024]{1,0:T(8,128)(2,1)S(1)} %multiply_convert_fusion.2, bf16[128,1024]{1,0:T(8,128)(2,1)} %param.12, f32[32,8,3,128]{3,2,1,0:T(4,128)S(1)} %bitcast.25), kind=kOutput, calls=%fused_computation.2 | convolution fusion | flops 1210580992 | bytes 1703936 | tf_op jit(solution)/shard_map/dot_general | solution.py:59
  14.6 0.0 copy-start.1
  14.6 25.8 %all-gather.2.cloned.1.call-done = bf16[1024,1024]{1,0:T(8,128)(2,1)} async-done(((bf16[128,1024]{1,0:T(8,128)(2,1)}), bf16[1024,1024]{1,0:T(8,128)(2,1)}) %all-gather.2.cloned.1.call-update) | async-done | bytes 2097168 | tf_op jit(solution)/shard_map/all_gather | solution.py:63
  40.4 3.2 %multiply_convert_fusion.1 = (bf16[256,1024]{1,0:T(8,128)(2,1)}, f32[256,1024]{1,0:T(8,128)S(1)}) fusion(bf16[256,1024]{1,0:T(8,128)(2,1)S(1)} %convolution_convert_fusion, bf16[1024,1024]{1,0:T(8,128)(2,1)} %all-gather.2.cloned.1.call-done), kind=kOutput, calls=%fused_computation.6 | convolution fusion | flops 538181632 | bytes 4194304 | tf_op jit(solution)/shard_map/dot_general | solution.py:61
  43.6 0.0 copy-done.1
  43.6 2.9 %fusion.19 = f32[1024,1024]{1,0:T(8,128)} fusion(bf16[256,1024]{1,0:T(8,128)(2,1)S(1)} %convolution_convert_fusion, f32[256,1024]{1,0:T(8,128)S(1)} %get-tuple-element.6, bf16[256,1024]{1,0:T(8,128)(2,1)S(1)} %copy-done.1), kind=kOutput, calls=%fused_computation.39 | convolution fusion | flops 539492352 | bytes 6291456 | tf_op jit(solution)/shard_map/dot_general | solution.py:76
  46.5 0.0 copy-start.3
  46.5 0.0 copy-start.2
  46.5 0.0 reduce-scatter.2.cloned.1.call-update
  46.5 0.7 copy-done.3
  47.1 0.1 reshape.86
  47.2 0.2 copy-done.2
  47.5 0.9 gather_fusion
  48.3 0.8 broadcast_select_fusion
  49.1 3.4 %all-to-all-start = ((bf16[8,16,1024]{2,1,0:T(8,128)(2,1)}), bf16[8,16,1024]{2,1,0:T(8,128)(2,1)S(1)}, u32[]{:S(2)}, u32[]{:S(2)}) async-start(bf16[8,16,1024]{2,1,0:T(8,128)(2,1)} %broadcast_select_fusion), calls=%async_computation.1 | async-start | bytes 524288 | tf_op jit(solution)/shard_map/all_to_all | solution.py:47
  52.5 0.0 all-reduce.2.cloned.1.call-start
  52.6 0.1 eq.48
  52.7 6.7 %all-to-all-done = bf16[8,16,1024]{2,1,0:T(8,128)(2,1)S(1)} async-done(((bf16[8,16,1024]{2,1,0:T(8,128)(2,1)}), bf16[8,16,1024]{2,1,0:T(8,128)(2,1)S(1)}, u32[]{:S(2)}, u32[]{:S(2)}) %all-to-all-start) | async-done | bytes 262176 | tf_op jit(solution)/shard_map/all_to_all | solution.py:47
  59.4 3.3 %convolution_convert_fusion.1 = bf16[256,1024]{1,0:T(8,128)(2,1)} fusion(bf16[1024,1024]{1,0:T(8,128)(2,1)} %all-gather.2.cloned.1.call-done, f32[256,1024]{1,0:T(8,128)S(1)} %get-tuple-element.6, bf16[256,1024]{1,0:T(8,128)(2,1)S(1)} %copy-done.1), kind=kOutput, calls=%fused_computation.4 | convolution fusion | flops 539754496 | bytes 4194304 | tf_op jit(solution)/shard_map/dot_general | solution.py:69
  62.7 35.0 %reduce-scatter.2.cloned.1.call-done = f32[128,1024]{1,0:T(8,128)} async-done(((f32[1024,1024]{1,0:T(8,128)}), f32[128,1024]{1,0:T(8,128)}) %reduce-scatter.2.cloned.1.call-update) | async-done | bytes 524304 | tf_op jit(solution)/shard_map/reduce_scatter | solution.py:79
  97.8 0.0 all-reduce.2.cloned.1.call-update
  97.8 1.9 %fusion.7 = f32[384,1024]{1,0:T(8,128)S(1)} fusion(bf16[256,1024]{1,0:T(8,128)(2,1)} %convolution_convert_fusion.1, f32[32,8,3,128]{3,2,1,0:T(4,128)S(1)} %bitcast.26), kind=kOutput, calls=%fused_computation.17 | convolution fusion | flops 1207959552 | bytes 2490368 | tf_op jit(solution)/shard_map/dot_general | solution.py:81
  99.7 0.7 slice.15
  100.4 3.4 %all-to-all-start.1 = ((bf16[8,16,1024]{2,1,0:T(8,128)(2,1)}), bf16[8,16,1024]{2,1,0:T(8,128)(2,1)S(1)}, u32[]{:S(2)}, u32[]{:S(2)}) async-start(bf16[8,16,1024]{2,1,0:T(8,128)(2,1)} %bitcast.6), calls=%async_computation.2 | async-start | bytes 524288 | tf_op jit(solution)/shard_map/all_to_all | solution.py:88
  103.8 0.0 copy-done
  103.8 1.1 fusion
  104.9 5.7 %all-to-all-done.1 = bf16[8,16,1024]{2,1,0:T(8,128)(2,1)S(1)} async-done(((bf16[8,16,1024]{2,1,0:T(8,128)(2,1)}), bf16[8,16,1024]{2,1,0:T(8,128)(2,1)S(1)}, u32[]{:S(2)}, u32[]{:S(2)}) %all-to-all-start.1) | async-done | bytes 262176 | tf_op jit(solution)/shard_map/all_to_all | solution.py:88
  110.7 28.1 %all-reduce.2.cloned.1.call-done = f32[128,1024]{1,0:T(8,128)} async-done(((f32[128,1024]{1,0:T(8,128)}), f32[128,1024]{1,0:T(8,128)}) %all-reduce.2.cloned.1.call-update) | async-done | bytes 524304 | tf_op jit(solution)/shard_map/psum | solution.py:80
  138.8 1.9 %copy.38 = f32[128,1024]{1,0:T(8,128)} copy(f32[128,1024]{1,0:T(8,128)} %all-reduce.2.cloned.1.call-done) | data formatting | bytes 1048576
  140.7 0.7 copy.39
  141.4 0.7 copy.40
  (4 shorter events, 0.1 us)
Async XLA Ops:
  7.2 96.7 %copy-start = (bf16[128,1024]{1,0:T(8,128)(2,1)S(1)}, bf16[128,1024]{1,0:T(8,128)(2,1)}, u32[]{:S(2)}) copy-start(bf16[128,1024]{1,0:T(8,128)(2,1)} %param.22) | copy-start | bytes 786436
  7.2 33.2 %all-gather.2.cloned.1.call-start = ((), (), s32[]{:S(2)}) async-start(), calls=%async_computation.3 | async-start | bytes 2359296 | tf_op jit(solution)/shard_map/all_gather | solution.py:63
  7.9 89.9 %reduce-scatter.2.cloned.1.call-start = ((), (), s32[]{:S(2)}) async-start(), calls=%async_computation.4 | async-start | bytes 4718592 | tf_op jit(solution)/shard_map/reduce_scatter | solution.py:79
  14.6 29.0 %copy-start.1 = (bf16[256,1024]{1,0:T(8,128)(2,1)S(1)}, bf16[256,1024]{1,0:T(8,128)(2,1)}, u32[]{:S(2)}) copy-start(bf16[256,1024]{1,0:T(8,128)(2,1)} %param.21) | copy-start | bytes 1572868
  46.5 0.7 copy-start.3
  46.5 1.0 copy-start.2
  49.1 10.3 %all-to-all-start = ((bf16[8,16,1024]{2,1,0:T(8,128)(2,1)}), bf16[8,16,1024]{2,1,0:T(8,128)(2,1)S(1)}, u32[]{:S(2)}, u32[]{:S(2)}) async-start(bf16[8,16,1024]{2,1,0:T(8,128)(2,1)} %broadcast_select_fusion), calls=%async_computation.1 | async-start | bytes 524288 | tf_op jit(solution)/shard_map/all_to_all | solution.py:47
  52.5 86.3 %all-reduce.2.cloned.1.call-start = ((), (), s32[]{:S(2)}) async-start(), calls=%async_computation.5 | async-start | bytes 1048576 | tf_op jit(solution)/shard_map/psum | solution.py:80
  100.4 10.3 %all-to-all-start.1 = ((bf16[8,16,1024]{2,1,0:T(8,128)(2,1)}), bf16[8,16,1024]{2,1,0:T(8,128)(2,1)S(1)}, u32[]{:S(2)}, u32[]{:S(2)}) async-start(bf16[8,16,1024]{2,1,0:T(8,128)(2,1)} %bitcast.6), calls=%async_computation.2 | async-start | bytes 524288 | tf_op jit(solution)/shard_map/all_to_all | solution.py:88
Sparse Core Ops, SparseCore 0:
  9.9 30.4 all-gather.1
  46.6 51.1 reduce-scatter.1
  100.1 38.6 all-reduce.1
where the time goes:
time: 149 us
  waiting for transfers between devices  102 us (68%)
  matrix products  15.3 us (10%)
  between operations  13.8 us (9%)
  starting transfers between devices  6.95 us (5%)
  local copies, waits for them, and re-layouts  5.91 us (4%)
  other arithmetic  4.51 us (3%)
    reduce_scatter x1, waiting for transfers between devices, local(): lax.psum_scatter(partial_value, 'dom', scatter_dimension=0, tiled=True)  35 us
    psum x1, waiting for transfers between devices, local(): weight_grad = lax.psum(block_sum, 'group')  28.1 us
    all_gather x1, waiting for transfers between devices, local(): lax.all_gather(weight, 'dom', axis=0, tiled=True)  25.8 us
    all_to_all x1, waiting for transfers between devices, local(): lax.all_to_all(outgoing, 'dom', split_axis=0, concat_axis=0, tiled=True)  6.71 us
    all_to_all x1, waiting for transfers between devices, local(): lax.all_to_all(bound_grad, 'dom', split_axis=0, concat_axis=0, tiled=True)  5.75 us
    unnamed x11, local copies, waits for them, and re-layouts  4.15 us
    all_to_all x1, starting transfers between devices, local(): lax.all_to_all(outgoing, 'dom', split_axis=0, concat_axis=0, tiled=True)  3.42 us
    all_to_all x1, starting transfers between devices, local(): lax.all_to_all(bound_grad, 'dom', split_axis=0, concat_axis=0, tiled=True)  3.41 us
  transfers between devices with their start and end apart: 5, of which 5 were waited for; matrix products, arithmetic and copies ran while one was open for 10% of the time, Pallas kernels for 0%

commit v1 on v0

--- a/solution.py
+++ b/solution.py
@@ -77,7 +77,7 @@
         hidden, pre_grad, (((0,), (0,)), ((), ())), preferred_element_type=jnp.float32
     )
     block_sum = lax.psum_scatter(partial_value, "dom", scatter_dimension=0, tiled=True)
-    weight_grad = lax.psum(block_sum, "group")
+    weight_grad = jnp.sum(lax.all_gather(block_sum, "group"), axis=0)
     src_grad = lax.dot_general(
         operator,
         hid_grad.astype(jnp.float32),

time: 149 us -> 156 us (1.047)
  waiting for transfers between devices: 102 us -> 111 us
  local copies, waits for them, and re-layouts: 5.91 us -> 3.19 us
  other arithmetic: 4.51 us -> 7.11 us
  matrix products: 15.3 us -> 13.4 us
    psum x1 -> x0, waiting for transfers between devices: 28.1 us -> none  [local(): weight_grad = lax.psum(block_sum, 'group')]
    all_gather x0 -> x1, waiting for transfers between devices: none -> 20.8 us  [local(): weight_grad = jnp.sum(lax.all_gather(block_sum, 'group'), axis=0)]
    reduce_scatter x1, waiting for transfers between devices: 35 us -> 51.2 us  [local(): lax.psum_scatter(partial_value, 'dom', scatter_dimension=0, tiled=True)]
    unnamed x11 -> x10, local copies, waits for them, and re-layouts: 4.15 us -> 1.43 us
    reduce_sum x0 -> x1, other arithmetic: none -> 2.59 us  [local(): weight_grad = jnp.sum(lax.all_gather(block_sum, 'group'), axis=0)]
  transfers between devices with their start and end apart: 5 -> 5, of which waited for: 5 -> 5; matrix products, arithmetic and copies ran while one was open for 10% -> 9% of each run, Pallas kernels for 0% -> 0%
where the time goes in v1:
time: 156 us
  waiting for transfers between devices  111 us (71%)
  between operations  13.9 us (9%)
  matrix products  13.4 us (9%)
  other arithmetic  7.11 us (5%)
  starting transfers between devices  6.94 us (4%)
  local copies, waits for them, and re-layouts  3.19 us (2%)
    reduce_scatter x1, waiting for transfers between devices, local(): lax.psum_scatter(partial_value, 'dom', scatter_dimension=0, tiled=True)  51.2 us
    all_gather x1, waiting for transfers between devices, local(): lax.all_gather(weight, 'dom', axis=0, tiled=True)  25.8 us
    all_gather x1, waiting for transfers between devices, local(): weight_grad = jnp.sum(lax.all_gather(block_sum, 'group'), axis=0)  20.8 us
    all_to_all x1, waiting for transfers between devices, local(): lax.all_to_all(outgoing, 'dom', split_axis=0, concat_axis=0, tiled=True)  6.76 us
    all_to_all x1, waiting for transfers between devices, local(): lax.all_to_all(bound_grad, 'dom', split_axis=0, concat_axis=0, tiled=True)  5.74 us
    all_to_all x1, starting transfers between devices, local(): lax.all_to_all(bound_grad, 'dom', split_axis=0, concat_axis=0, tiled=True)  3.41 us
    all_to_all x1, starting transfers between devices, local(): lax.all_to_all(outgoing, 'dom', split_axis=0, concat_axis=0, tiled=True)  3.41 us
    dot_general x1, matrix products, local(): jnp.dot(hidden, lax.all_gather(weight, 'dom', axis=0, tiled=True), prefer...  3.18 us
  transfers between devices with their start and end apart: 5, of which 5 were waited for; matrix products, arithmetic and copies ran while one was open for 9% of the time, Pallas kernels for 0%

profile of v1, /device:TPU:0, one launch (start us, length us, event | category | flops | bytes accessed | tf_op | source)
XLA Modules:
  0.0 155.6 jit_solution(9613588030354754084)
XLA Ops:
  7.2 0.0 copy-start
  7.2 0.0 all-gather.4.cloned.1.call-start
  7.2 0.7 all-gather.4.cloned.1.call-update
  7.9 0.0 reduce-scatter.2.cloned.1.call-start
  8.0 0.9 select_reduce_fusion
  8.8 0.7 iota_compare_fusion.4
  9.6 1.0 broadcast_select_fusion.1
  10.6 1.1 multiply_convert_fusion.2
  11.6 1.0 fusion.11
  12.6 2.0 %convolution_convert_fusion = bf16[256,1024]{1,0:T(8,128)(2,1)S(1)} fusion(bf16[128,1024]{1,0:T(8,128)(2,1)} %param.16, bf16[128,1024]{1,0:T(8,128)(2,1)S(1)} %multiply_convert_fusion.2, bf16[128,1024]{1,0:T(8,128)(2,1)} %param.12, f32[32,8,3,128]{3,2,1,0:T(4,128)S(1)} %bitcast.27), kind=kOutput, calls=%fused_computation.2 | convolution fusion | flops 1210580992 | bytes 1703936 | tf_op jit(solution)/shard_map/dot_general | solution.py:59
  14.6 0.0 copy-start.1
  14.6 25.8 %all-gather.4.cloned.1.call-done = bf16[1024,1024]{1,0:T(8,128)(2,1)} async-done(((bf16[128,1024]{1,0:T(8,128)(2,1)}), bf16[1024,1024]{1,0:T(8,128)(2,1)}) %all-gather.4.cloned.1.call-update) | async-done | bytes 2097168 | tf_op jit(solution)/shard_map/all_gather | solution.py:63
  40.4 3.2 %multiply_convert_fusion.1 = (bf16[256,1024]{1,0:T(8,128)(2,1)}, f32[256,1024]{1,0:T(8,128)S(1)}) fusion(bf16[256,1024]{1,0:T(8,128)(2,1)S(1)} %convolution_convert_fusion, bf16[1024,1024]{1,0:T(8,128)(2,1)} %all-gather.4.cloned.1.call-done), kind=kOutput, calls=%fused_computation.6 | convolution fusion | flops 538181632 | bytes 4194304 | tf_op jit(solution)/shard_map/dot_general | solution.py:61
  43.6 0.0 copy-done.1
  43.6 2.9 %fusion.19 = f32[1024,1024]{1,0:T(8,128)} fusion(bf16[256,1024]{1,0:T(8,128)(2,1)S(1)} %convolution_convert_fusion, f32[256,1024]{1,0:T(8,128)S(1)} %get-tuple-element.6, bf16[256,1024]{1,0:T(8,128)(2,1)S(1)} %copy-done.1), kind=kOutput, calls=%fused_computation.39 | convolution fusion | flops 539492352 | bytes 6291456 | tf_op jit(solution)/shard_map/dot_general | solution.py:76
  46.5 0.0 copy-start.3
  46.5 0.0 copy-start.2
  46.5 0.0 reduce-scatter.2.cloned.1.call-update
  46.5 0.0 all-gather.6.cloned.1.call-start
  46.5 51.2 %reduce-scatter.2.cloned.1.call-done = f32[128,1024]{1,0:T(8,128)} async-done(((f32[1024,1024]{1,0:T(8,128)}), f32[128,1024]{1,0:T(8,128)}) %reduce-scatter.2.cloned.1.call-update) | async-done | bytes 524304 | tf_op jit(solution)/shard_map/reduce_scatter | solution.py:79
  97.8 0.0 all-gather.6.cloned.1.call-update
  97.8 0.0 copy-done.3
  97.8 0.1 reshape.86
  97.9 0.0 copy-done.2
  98.0 0.9 gather_fusion
  98.8 0.8 broadcast_select_fusion
  99.6 3.4 %all-to-all-start = ((bf16[8,16,1024]{2,1,0:T(8,128)(2,1)}), bf16[8,16,1024]{2,1,0:T(8,128)(2,1)S(1)}, u32[]{:S(2)}, u32[]{:S(2)}) async-start(bf16[8,16,1024]{2,1,0:T(8,128)(2,1)} %broadcast_select_fusion), calls=%async_computation.1 | async-start | bytes 524288 | tf_op jit(solution)/shard_map/all_to_all | solution.py:47
  103.1 0.1 eq.48
  103.1 6.8 %all-to-all-done = bf16[8,16,1024]{2,1,0:T(8,128)(2,1)S(1)} async-done(((bf16[8,16,1024]{2,1,0:T(8,128)(2,1)}), bf16[8,16,1024]{2,1,0:T(8,128)(2,1)S(1)}, u32[]{:S(2)}, u32[]{:S(2)}) %all-to-all-start) | async-done | bytes 262176 | tf_op jit(solution)/shard_map/all_to_all | solution.py:47
  109.9 2.5 %convolution_convert_fusion.1 = bf16[256,1024]{1,0:T(8,128)(2,1)S(1)} fusion(bf16[1024,1024]{1,0:T(8,128)(2,1)} %all-gather.4.cloned.1.call-done, f32[256,1024]{1,0:T(8,128)S(1)} %get-tuple-element.6, bf16[256,1024]{1,0:T(8,128)(2,1)S(1)} %copy-done.1), kind=kOutput, calls=%fused_computation.4 | convolution fusion | flops 539754496 | bytes 4194304 | tf_op jit(solution)/shard_map/dot_general | solution.py:69
  112.4 0.8 fusion.7
  113.2 0.7 slice.15
  113.9 3.4 %all-to-all-start.1 = ((bf16[8,16,1024]{2,1,0:T(8,128)(2,1)}), bf16[8,16,1024]{2,1,0:T(8,128)(2,1)S(1)}, u32[]{:S(2)}, u32[]{:S(2)}) async-start(bf16[8,16,1024]{2,1,0:T(8,128)(2,1)} %bitcast.7), calls=%async_computation.2 | async-start | bytes 524288 | tf_op jit(solution)/shard_map/all_to_all | solution.py:88
  117.4 0.0 copy-done
  117.4 1.1 fusion
  118.5 5.7 %all-to-all-done.1 = bf16[8,16,1024]{2,1,0:T(8,128)(2,1)S(1)} async-done(((bf16[8,16,1024]{2,1,0:T(8,128)(2,1)}), bf16[8,16,1024]{2,1,0:T(8,128)(2,1)S(1)}, u32[]{:S(2)}, u32[]{:S(2)}) %all-to-all-start.1) | async-done | bytes 262176 | tf_op jit(solution)/shard_map/all_to_all | solution.py:88
  124.2 20.8 %all-gather.6.cloned.1.call-done = f32[512,1024]{1,0:T(8,128)} async-done(((f32[128,1024]{1,0:T(8,128)}), f32[512,1024]{1,0:T(8,128)}) %all-gather.6.cloned.1.call-update) | async-done | bytes 2097168 | tf_op jit(solution)/shard_map/all_gather | solution.py:80
  145.0 2.6 %reduce_sum.19 = f32[128,1024]{1,0:T(8,128)} reduce(f32[4,128,1024]{2,1,0:T(8,128)} %bitcast.26, f32[]{:T(128)} %constant.8.clone.1), dimensions={0}, to_apply=%region_2.3 | reduce | flops 393216 | bytes 2621444 | tf_op jit(solution)/shard_map/reduce_sum | solution.py:80
  147.6 0.7 copy.37
  148.3 0.7 copy.38
  (4 shorter events, 0.1 us)
Async XLA Ops:
  7.2 110.2 %copy-start = (bf16[128,1024]{1,0:T(8,128)(2,1)S(1)}, bf16[128,1024]{1,0:T(8,128)(2,1)}, u32[]{:S(2)}) copy-start(bf16[128,1024]{1,0:T(8,128)(2,1)} %param.22) | copy-start | bytes 786436
  7.2 33.2 %all-gather.4.cloned.1.call-start = ((), (), s32[]{:S(2)}) async-start(), calls=%async_computation.3 | async-start | bytes 2359296 | tf_op jit(solution)/shard_map/all_gather | solution.py:63
  7.9 89.9 %reduce-scatter.2.cloned.1.call-start = ((), (), s32[]{:S(2)}) async-start(), calls=%async_computation.4 | async-start | bytes 4718592 | tf_op jit(solution)/shard_map/reduce_scatter | solution.py:79
  14.6 29.0 %copy-start.1 = (bf16[256,1024]{1,0:T(8,128)(2,1)S(1)}, bf16[256,1024]{1,0:T(8,128)(2,1)}, u32[]{:S(2)}) copy-start(bf16[256,1024]{1,0:T(8,128)(2,1)} %param.21) | copy-start | bytes 1572868
  46.5 51.3 %copy-start.3 = (s32[8,16]{1,0:T(8,128)S(1)}, s32[8,16]{1,0:T(8,128)}, u32[]{:S(2)}) copy-start(s32[8,16]{1,0:T(8,128)} %param.23) | copy-start | bytes 1540
  46.5 51.5 %copy-start.2 = (bf16[128,1024]{1,0:T(8,128)(2,1)S(1)}, bf16[128,1024]{1,0:T(8,128)(2,1)}, u32[]{:S(2)}) copy-start(bf16[128,1024]{1,0:T(8,128)(2,1)} %param.12) | copy-start | bytes 786436
  46.5 98.6 %all-gather.6.cloned.1.call-start = ((), (), s32[]{:S(2)}) async-start(), calls=%async_computation.5 | async-start | bytes 2621440 | tf_op jit(solution)/shard_map/all_gather | solution.py:80
  99.6 10.3 %all-to-all-start = ((bf16[8,16,1024]{2,1,0:T(8,128)(2,1)}), bf16[8,16,1024]{2,1,0:T(8,128)(2,1)S(1)}, u32[]{:S(2)}, u32[]{:S(2)}) async-start(bf16[8,16,1024]{2,1,0:T(8,128)(2,1)} %broadcast_select_fusion), calls=%async_computation.1 | async-start | bytes 524288 | tf_op jit(solution)/shard_map/all_to_all | solution.py:47
  113.9 10.3 %all-to-all-start.1 = ((bf16[8,16,1024]{2,1,0:T(8,128)(2,1)}), bf16[8,16,1024]{2,1,0:T(8,128)(2,1)S(1)}, u32[]{:S(2)}, u32[]{:S(2)}) async-start(bf16[8,16,1024]{2,1,0:T(8,128)(2,1)} %bitcast.7), calls=%async_computation.2 | async-start | bytes 524288 | tf_op jit(solution)/shard_map/all_to_all | solution.py:88
Sparse Core Ops, SparseCore 0:
  9.9 30.4 all-gather.3
  46.6 51.1 reduce-scatter.1
  99.4 45.6 all-gather.5
